TPU v7x, 32 devices: a whole 2x2x4 slice. The times are simulated.
32 devices in a mesh: grp: 2 (over x), inp: 4 (over y, core), tm: 4 (over z).
Axes of the slice: x: 2, y: 2, z: 4, core: 2. Of those that a mesh axis runs over, the one named last changes fastest.
Arguments:
- samples: bfloat16 [64, 1024, 8192], P(('grp', 'tm'), 'inp'), parts along dimension 0, may hold values from -6 to 6
- fir: float32 [16, 8192], replicated, may hold values from -1 to 1
- flags: int32 [64, 1024], P(('grp', 'tm'), 'inp'), parts along dimension 0, may hold values 0 or 1
Outputs:
- visibilities: float32 [16, 2, 1024, 1024], P(('grp', 'tm'), None, 'inp'), parts along dimension 0
There are 2 independent parts, one for each index of `grp`. A program takes and returns all parts, laid end to end along the dimension named above; an argument that names none is the same for every part. Nothing has to cross between parts.
All inputs are finite; a program needn't handle non-finite values. No bound on the sum of `flags` on one device may be relied on, other than what follows from the above.
Results may differ from a plain program's by a relative error of at most 0.0063.
Values may be sent and summed in bfloat16 or wider, within the bound.
A program may use at most 256 MiB of HBM per device.

v0:
```python
import functools
import math

import jax
import jax.numpy as jnp
from jax import lax
from jax.experimental import pallas as pl
from jax.experimental.pallas import tpu as pltpu
from jax.sharding import PartitionSpec as P

NCH = 4096
CH_DEV = 2
STRIP = 1024
ROWS = 128


def channelize(tms, inps, fir_hbm, flags_ref, x_hbm, all_ref, fir_buf, x_buf, weights, total,
               part_out, part_in, flag_out, flag_in, fir_sem, x_sem, flag_sems, part_sems, all_sems):
    pieces, strips, frames, rows, strip = x_buf.shape
    taps, length = fir_buf.shape
    blocks = part_in.shape[2] // (2 * CH_DEV * frames)
    window = 2 * taps
    my_tm, my_inp = lax.axis_index("tm"), lax.axis_index("inp")

    def x_copy(piece, at):
        return pltpu.make_async_copy(
            x_hbm.at[:, pl.ds(piece * rows, rows), pl.ds(pl.multiple_of(at * strip, strip), strip)],
            x_buf.at[piece, at], x_sem.at[piece, at])

    def turn(axis, count, step):
        return {axis: lax.rem(lax.axis_index(axis) + step, count)}

    fir_copy = pltpu.make_async_copy(fir_hbm, fir_buf, fir_sem)
    fir_copy.start()
    for piece in range(pieces):
        for at in range(strips):
            x_copy(piece, at).start()

    barrier = pltpu.get_barrier_semaphore()
    for axis, count in (("tm", tms), ("inp", inps)):
        for step in range(1, count):
            pl.semaphore_signal(barrier, inc=1, device_id=turn(axis, count, step), device_id_type=pl.DeviceIdType.MESH)

    row = lax.broadcasted_iota(jnp.int32, (frames, frames), 0)
    col = lax.broadcasted_iota(jnp.int32, (frames, frames), 1)
    mirror = (row + col == frames - 1).astype(jnp.float32)
    mirrored = jnp.dot(mirror, flags_ref[...].astype(jnp.float32), preferred_element_type=jnp.float32)
    flag_out[...] = mirrored
    flag_in[my_tm] = mirrored

    group_count = tms * 2 * CH_DEV
    fir_copy.wait()

    def build(at, carry):
        group = lax.broadcasted_iota(jnp.int32, (group_count, strip), 0)
        sample = at * strip + lax.broadcasted_iota(jnp.int32, (group_count, strip), 1)
        slab = (group // (4 * CH_DEV)) * 2 + group % 2
        channel = NCH // 4 + slab * CH_DEV + (group // 4) % CH_DEV
        quarter = (group // 2) % 2
        phase = jnp.bitwise_and(sample * channel + quarter * (length // 4), length - 1)
        table = math.sqrt(2.0 / length) * jnp.cos((2.0 * math.pi / length) * phase.astype(jnp.float32))
        table = table.astype(jnp.bfloat16).astype(jnp.float32)
        fir = fir_buf[:, pl.ds(pl.multiple_of(at * strip, strip), strip)]
        for g in range(group_count):
            weights[at, g * taps:(g + 1) * taps, :] = (fir * table[g:g + 1, :]).astype(jnp.bfloat16)
        return carry

    lax.fori_loop(0, strips, build, 0)

    pl.semaphore_wait(barrier, tms + inps - 2)
    flag_copies = []
    for step in range(1, tms):
        copy = pltpu.make_async_remote_copy(
            flag_out, flag_in.at[my_tm], flag_sems.at[0, step - 1], flag_sems.at[1, step - 1],
            device_id=turn("tm", tms, step), device_id_type=pl.DeviceIdType.MESH)
        copy.start()
        flag_copies.append(copy)

    def multiply(piece, first, last):
        def step(at, carry):
            x_copy(piece, at).wait()
            voltages = x_buf[piece, at].reshape(frames * rows, strip)
            product = lax.dot_general(voltages, weights[at], (((1,), (1,)), ((), ())), preferred_element_type=jnp.float32)
            total[...] = jnp.where(at == 0, product, total[...] + product)
            return carry
        lax.fori_loop(first, last, step, 0)

    def send_parts(piece):
        lane = lax.broadcasted_iota(jnp.int32, (rows, 4 * CH_DEV * taps), 1)
        for slab in range(tms):
            pair, half = slab // 2, slab % 2
            kept = (lane // taps) % 2 == half
            at = slice(pair * 4 * CH_DEV * taps, (pair + 1) * 4 * CH_DEV * taps)
            value = None
            for s in range(frames):
                own = jnp.where(kept, total[s * rows:(s + 1) * rows, at], 0.0)
                value = own if value is None else value + own
                shift = 1 if s < frames - 1 or half == 0 else lane.shape[1] + 1 - taps
                value = pltpu.roll(value, shift, 1)
            turned = value.T
            ordered = [turned[q * window + (blocks - 1 - h) * frames:q * window + (blocks - h) * frames]
                       for h in range(blocks) for q in range(2 * CH_DEV)]
            part_out[piece, slab] = jnp.concatenate(ordered, axis=0).astype(jnp.bfloat16)
        part_in[piece, my_tm] = part_out[piece, my_tm]
        copies = []
        for step in range(1, tms):
            to = turn("tm", tms, step)
            copy = pltpu.make_async_remote_copy(
                part_out.at[piece, to["tm"]], part_in.at[piece, my_tm],
                part_sems.at[0, piece, step - 1], part_sems.at[1, piece, step - 1],
                device_id=to, device_id_type=pl.DeviceIdType.MESH)
            copy.start()
            copies.append(copy)
        return copies

    def gather(piece, part_copies):
        for copy in part_copies:
            copy.wait_recv()
        columns = slice(piece * rows, (piece + 1) * rows)
        per = 2 * CH_DEV * frames
        for block in range(tms):
            value = None
            for h in range(min(blocks, block + 1)):
                term = part_in[piece, block - h, h * per:(h + 1) * per, :].astype(jnp.float32)
                value = term if value is None else value + term
            good = flag_in[block, :, columns]
            value = value * jnp.concatenate([good] * (2 * CH_DEV), axis=0)
            all_ref[my_inp, block * per:(block + 1) * per, columns] = value.astype(jnp.bfloat16)
        copies = []
        for step in range(1, inps):
            copy = pltpu.make_async_remote_copy(
                all_ref.at[my_inp, :, columns], all_ref.at[my_inp, :, columns],
                all_sems.at[0, piece, step - 1], all_sems.at[1, piece, step - 1],
                device_id=turn("inp", inps, step), device_id_type=pl.DeviceIdType.MESH)
            copy.start()
            copies.append(copy)
        return copies

    waiting, before = list(flag_copies), None
    for piece in range(pieces):
        middle = strips // 2 if before is not None else 0
        multiply(piece, 0, middle)
        if before is not None:
            if piece == 1:
                for copy in flag_copies:
                    copy.wait_recv()
            waiting += before
            got = gather(piece - 1, before)
            waiting += got
        multiply(piece, middle, strips)
        before = send_parts(piece)
    if pieces == 1:
        for copy in flag_copies:
            copy.wait_recv()
    waiting += before
    waiting += gather(pieces - 1, before)
    gathers = [copy for copy in waiting]
    for copy in gathers:
        copy.wait_send()
    return [copy for copy in waiting]


def channelize_body(tms, inps, *refs):
    pieces = refs[5].shape[0]
    waiting = channelize(tms, inps, *refs)
    flag_count, part_count, all_count = tms - 1, tms - 1, inps - 1
    at = flag_count
    for piece in range(pieces):
        at += part_count
        for copy in waiting[at:at + all_count]:
            copy.wait_recv()
        at += all_count


def correlate(inps, scale, all_ref, out_ref, sides):
    channel, part = pl.program_id(0), pl.program_id(1)
    rows = all_ref.shape[2]
    lane = lax.broadcasted_iota(jnp.int32, sides.shape[1:], 1)
    per = sides.shape[2] // scale[1]

    @pl.when(jnp.logical_and(channel == 0, part == 0))
    def _():
        own = all_ref[lax.axis_index("inp")].astype(jnp.float32).T
        size = own.shape[1]
        sides[0] = own
        sides[1] = jnp.where((lane // per) % 2 == 0, pltpu.roll(own, size - per, 1), -pltpu.roll(own, per, 1))

    side = jnp.where((lane // (2 * per)) % CH_DEV == channel, sides[part], 0.0).astype(jnp.bfloat16)
    for peer in range(inps):
        value = jnp.dot(side, all_ref[peer], preferred_element_type=jnp.float32)
        out_ref[0, 0, :, peer * rows:(peer + 1) * rows] = value * scale[0]


def shards(samples, fir, flags):
    frames, inputs, length = samples.shape
    taps = fir.shape[0]
    tms, inps = lax.axis_size("tm"), lax.axis_size("inp")
    blocks = (taps + frames - 2) // frames + 1
    assert length & (length - 1) == 0 and tms % 2 == 0 and blocks * frames <= 2 * taps
    rows = min(inputs, ROWS)
    pieces, strips = inputs // rows, length // STRIP
    columns = tms * 2 * CH_DEV * taps
    per = 2 * CH_DEV * frames
    vmem = pl.BlockSpec(memory_space=pltpu.VMEM)
    anywhere = pl.BlockSpec(memory_space=pl.ANY)
    every = pl.pallas_call(
        functools.partial(channelize_body, tms, inps),
        out_shape=jax.ShapeDtypeStruct((inps, tms * per, inputs), jnp.bfloat16),
        in_specs=[anywhere, vmem, anywhere],
        out_specs=vmem,
        scratch_shapes=[
            pltpu.VMEM((taps, length), jnp.float32),
            pltpu.VMEM((pieces, strips, frames, rows, STRIP), jnp.bfloat16),
            pltpu.VMEM((strips, columns, STRIP), jnp.bfloat16),
            pltpu.VMEM((frames * rows, columns), jnp.float32),
            pltpu.VMEM((pieces, tms, blocks * per, rows), jnp.bfloat16),
            pltpu.VMEM((pieces, tms, blocks * per, rows), jnp.bfloat16),
            pltpu.VMEM((frames, inputs), jnp.float32),
            pltpu.VMEM((tms, frames, inputs), jnp.float32),
            pltpu.SemaphoreType.DMA,
            pltpu.SemaphoreType.DMA((pieces, strips)),
            pltpu.SemaphoreType.DMA((2, tms - 1)),
            pltpu.SemaphoreType.DMA((2, pieces, tms - 1)),
            pltpu.SemaphoreType.DMA((2, pieces, inps - 1)),
        ],
        compiler_params=pltpu.CompilerParams(collective_id=0, has_side_effects=True, vmem_limit_bytes=60 << 20),
        name="channelize",
    )(fir, flags, samples)
    return pl.pallas_call(
        functools.partial(correlate, inps, (1.0 / (frames * tms), 2 * CH_DEV * tms)),
        out_shape=jax.ShapeDtypeStruct((CH_DEV, 2, inputs, inps * inputs), jnp.float32),
        grid=(CH_DEV, 2),
        in_specs=[pl.BlockSpec((inps, tms * per, inputs), lambda c, p: (0, 0, 0))],
        out_specs=pl.BlockSpec((1, 1, inputs, inps * inputs), lambda c, p: (c, p, 0, 0)),
        scratch_shapes=[pltpu.VMEM((2, inputs, tms * per), jnp.float32)],
        name="correlate",
    )(every)


def solution(mesh):
    in_specs = (P(("grp", "tm"), "inp", None), P(), P(("grp", "tm"), "inp"))
    out_specs = P(("grp", "tm"), None, "inp", None)
    return jax.shard_map(shards, mesh=mesh, in_specs=in_specs, out_specs=out_specs, check_vma=False)
```

profile of v0, /device:TPU:0, one launch (start us, length us, event | category | flops | bytes accessed | tf_op | source)
XLA Modules:
  0.0 33.9 jit_solution(4698986769842450427)
XLA Ops:
  0.0 29.9 %channelize.1.all_ref = bf16[4,128,256]{2,1,0:T(8,128)(2,1)} custom-call(f32[16,8192]{1,0:T(8,128)} %refs_0_.1, s32[8,256]{1,0:T(8,128)} %refs_1_.1, bf16[8,256,8192]{2,1,0:T(8,128)(2,1)} %refs_2_.1), custom_call_target="tpu_custom_call" | custom-call | tf_op jit(solution)/shard_map/channelize/pallas_call | solution.py:206
  29.9 4.0 %correlate.1 = f32[2,2,256,1024]{3,2,1,0:T(8,128)} custom-call(bf16[4,128,256]{2,1,0:T(8,128)(2,1)} %channelize.1.all_ref), custom_call_target="tpu_custom_call" | custom-call | tf_op jit(solution)/shard_map/correlate/pallas_call | solution.py:229
where the time goes:
time: 34.1 us; the launch traced here: 33.9 us
  Pallas kernels  33.9 us (99%)
    pallas_call x1, Pallas kernels, shards(): pl.pallas_call(functools.partial(channelize_body, tms, inps), out_shape=j...  29.9 us
    pallas_call x1, Pallas kernels, shards(): pl.pallas_call(functools.partial(correlate, inps, (1.0 / (frames * tms),...  4.04 us

commit v1 on v0

v1 whole, which is shorter than its diff:
```python
import functools
import math

import jax
import jax.numpy as jnp
from jax import lax
from jax.experimental import pallas as pl
from jax.experimental.pallas import tpu as pltpu
from jax.sharding import PartitionSpec as P

NCH = 4096
CH_DEV = 2
STRIP = 1024
ROWS = 128


def channelize(tms, inps, fir_hbm, flags_ref, x_hbm, all_ref, fir_buf, x_buf, weights, total,
               part_out, part_in, flag_out, flag_in, turns, fir_sem, x_sem, flag_sems, part_sems, all_sems):
    pieces, strips, frames, rows, strip = x_buf.shape
    taps, length = fir_buf.shape
    blocks = part_in.shape[2] // (2 * CH_DEV * frames)
    window = 2 * taps
    my_tm, my_inp = lax.axis_index("tm"), lax.axis_index("inp")

    def x_copy(piece, at):
        return pltpu.make_async_copy(
            x_hbm.at[:, pl.ds(piece * rows, rows), pl.ds(pl.multiple_of(at * strip, strip), strip)],
            x_buf.at[piece, at], x_sem.at[piece, at])

    def turn(axis, count, step):
        return {axis: lax.rem(lax.axis_index(axis) + step, count)}

    fir_copy = pltpu.make_async_copy(fir_hbm, fir_buf, fir_sem)
    fir_copy.start()
    for piece in range(pieces):
        for at in range(strips):
            x_copy(piece, at).start()

    barrier = pltpu.get_barrier_semaphore()
    for axis, count in (("tm", tms), ("inp", inps)):
        for step in range(1, count):
            pl.semaphore_signal(barrier, inc=1, device_id=turn(axis, count, step), device_id_type=pl.DeviceIdType.MESH)

    row = lax.broadcasted_iota(jnp.int32, (frames, frames), 0)
    col = lax.broadcasted_iota(jnp.int32, (frames, frames), 1)
    mirror = (row + col == frames - 1).astype(jnp.float32)
    mirrored = jnp.dot(mirror, flags_ref[...].astype(jnp.float32), preferred_element_type=jnp.float32)
    flag_out[...] = mirrored
    flag_in[my_tm] = mirrored

    group_count = tms * 2 * CH_DEV

    def channel_of(shape):
        group = lax.broadcasted_iota(jnp.int32, shape, 0)
        slab = (group // (4 * CH_DEV)) * 2 + group % 2
        return NCH // 4 + slab * CH_DEV + (group // 4) % CH_DEV, (group // 2) % 2

    def cosine(phase):
        return jnp.cos((2.0 * math.pi / length) * jnp.bitwise_and(phase, length - 1).astype(jnp.float32))

    channel, quarter = channel_of((group_count, strip))
    phase = lax.broadcasted_iota(jnp.int32, (group_count, strip), 1) * channel + quarter * (length // 4)
    factor = math.sqrt(2.0 / length)
    turns[0] = factor * cosine(phase)
    turns[1] = factor * cosine(phase - length // 4)
    channel, _ = channel_of((group_count, 128))
    step_phase = lax.broadcasted_iota(jnp.int32, (group_count, 128), 1) * strip * channel
    turn_cos, turn_sin = cosine(step_phase), cosine(step_phase - length // 4)
    fir_copy.wait()

    for at in range(strips):
        table = turns[0] * turn_cos[:, at:at + 1] - turns[1] * turn_sin[:, at:at + 1]
        table = table.astype(jnp.bfloat16).astype(jnp.float32)
        fir = fir_buf[:, at * strip:(at + 1) * strip]
        for g in range(group_count):
            weights[at, g * taps:(g + 1) * taps, :] = (fir * table[g:g + 1, :]).astype(jnp.bfloat16)

    def send_flags():
        pl.semaphore_wait(barrier, tms + inps - 2)
        copies = []
        for step in range(1, tms):
            copy = pltpu.make_async_remote_copy(
                flag_out, flag_in.at[my_tm], flag_sems.at[0, step - 1], flag_sems.at[1, step - 1],
                device_id=turn("tm", tms, step), device_id_type=pl.DeviceIdType.MESH)
            copy.start()
            copies.append(copy)
        return copies

    def multiply(piece):
        def add(at, carry):
            x_copy(piece, at).wait()
            voltages = x_buf[piece, at].reshape(frames * rows, strip)
            product = lax.dot_general(voltages, weights[at], (((1,), (1,)), ((), ())), preferred_element_type=jnp.float32)
            total[...] = jnp.where(at == 0, product, total[...] + product)
            return carry
        lax.fori_loop(0, strips, add, 0)

    def part_copy(piece, slot, to):
        return pltpu.make_async_remote_copy(
            part_out.at[piece, to], part_in.at[piece, slot], part_sems.at[0, piece, to], part_sems.at[1, piece, slot],
            device_id={"tm": to}, device_id_type=pl.DeviceIdType.MESH)

    def send_parts(piece):
        wide, room, pairs = 4 * CH_DEV * taps, blocks * frames - taps, tms // 2
        place = lax.broadcasted_iota(jnp.int32, (rows, wide), 1) % window
        my_pair, my_half = my_tm // 2, lax.rem(my_tm, 2)
        for ahead in range(1, pairs + 1):
            pair = lax.rem(my_pair + ahead, pairs)
            lanes = pl.ds(pl.multiple_of(pair * wide, wide), wide)
            first = second = None
            for s in range(frames):
                moved = pltpu.roll(total[s * rows:(s + 1) * rows, lanes], room - s, 1)
                inside = jnp.logical_and(place >= room - s, place < room - s + taps)
                one, two = jnp.where(inside, moved, 0.0), jnp.where(inside, 0.0, moved)
                first, second = (one, two) if s == 0 else (first + one, second + two)
            for half, value in enumerate((first, pltpu.roll(second, wide - taps, 1))):
                turned = value.T
                ordered = [turned[q * window + (blocks - 1 - h) * frames:q * window + (blocks - h) * frames]
                           for h in range(blocks) for q in range(2 * CH_DEV)]
                part_out[piece, 2 * pair + half] = jnp.concatenate(ordered, axis=0).astype(jnp.bfloat16)
                if ahead < pairs:
                    part_copy(piece, my_tm, 2 * pair + half).start()
        part_copy(piece, my_tm, 2 * my_pair + 1 - my_half).start()
        part_in[piece, my_tm] = part_out[piece, my_tm]

    def gather(piece):
        for step in range(1, tms):
            source = lax.rem(my_tm + step, tms)
            part_copy(piece, source, source).wait_recv()
        columns = slice(piece * rows, (piece + 1) * rows)
        per = 2 * CH_DEV * frames
        for block in range(tms):
            value = None
            for h in range(min(blocks, block + 1)):
                term = part_in[piece, block - h, h * per:(h + 1) * per, :].astype(jnp.float32)
                value = term if value is None else value + term
            good = flag_in[block, :, columns]
            value = value * jnp.concatenate([good] * (2 * CH_DEV), axis=0)
            all_ref[my_inp, block * per:(block + 1) * per, columns] = value.astype(jnp.bfloat16)
        copies = []
        for step in range(1, inps):
            copy = pltpu.make_async_remote_copy(
                all_ref.at[my_inp, :, columns], all_ref.at[my_inp, :, columns],
                all_sems.at[0, piece, step - 1], all_sems.at[1, piece, step - 1],
                device_id=turn("inp", inps, step), device_id_type=pl.DeviceIdType.MESH)
            copy.start()
            copies.append(copy)
        return copies

    flag_copies, all_copies = [], []

    def gather_after(piece):
        if piece == 0:
            for copy in flag_copies:
                copy.wait_recv()
        all_copies.extend(gather(piece))

    for piece in range(pieces):
        multiply(piece)
        if piece == 0:
            flag_copies.extend(send_flags())
        send_parts(piece)
        if piece > 0:
            gather_after(piece - 1)
    gather_after(pieces - 1)
    for copy in all_copies:
        copy.wait_recv()
    for copy in flag_copies + all_copies:
        copy.wait_send()
    for piece in range(pieces):
        for step in range(1, tms):
            to = lax.rem(my_tm + step, tms)
            part_copy(piece, my_tm, to).wait_send()


def correlate(inps, scale, all_ref, out_ref, sides, stage, sems):
    rows = all_ref.shape[2]
    own = all_ref[lax.axis_index("inp")].astype(jnp.float32).T * scale[0]
    size = own.shape[1]
    per = size // scale[1]
    lane = lax.broadcasted_iota(jnp.int32, own.shape, 1)
    sides[0] = own
    sides[1] = jnp.where((lane // per) % 2 == 0, pltpu.roll(own, size - per, 1), -pltpu.roll(own, per, 1))
    copies = []
    for channel in range(CH_DEV):
        for part in range(2):
            side = jnp.where((lane // (2 * per)) % CH_DEV == channel, sides[part], 0.0).astype(jnp.bfloat16)
            for peer in range(inps):
                columns = slice(peer * rows, (peer + 1) * rows)
                stage[channel, part, :, columns] = jnp.dot(side, all_ref[peer], preferred_element_type=jnp.float32)
            copy = pltpu.make_async_copy(stage.at[channel, part], out_ref.at[channel, part], sems.at[channel, part])
            copy.start()
            copies.append(copy)
    for copy in copies:
        copy.wait()


def shards(samples, fir, flags):
    frames, inputs, length = samples.shape
    taps = fir.shape[0]
    tms, inps = lax.axis_size("tm"), lax.axis_size("inp")
    blocks = (taps + frames - 2) // frames + 1
    assert length // STRIP <= 128 and length & (length - 1) == 0 and tms % 2 == 0 and blocks * frames <= 2 * taps
    rows = min(inputs, ROWS)
    pieces, strips = inputs // rows, length // STRIP
    columns = tms * 2 * CH_DEV * taps
    per = 2 * CH_DEV * frames
    vmem = pl.BlockSpec(memory_space=pltpu.VMEM)
    anywhere = pl.BlockSpec(memory_space=pl.ANY)
    every = pl.pallas_call(
        functools.partial(channelize, tms, inps),
        out_shape=jax.ShapeDtypeStruct((inps, tms * per, inputs), jnp.bfloat16),
        in_specs=[anywhere, vmem, anywhere],
        out_specs=vmem,
        scratch_shapes=[
            pltpu.VMEM((taps, length), jnp.float32),
            pltpu.VMEM((pieces, strips, frames, rows, STRIP), jnp.bfloat16),
            pltpu.VMEM((strips, columns, STRIP), jnp.bfloat16),
            pltpu.VMEM((frames * rows, columns), jnp.float32),
            pltpu.VMEM((pieces, tms, blocks * per, rows), jnp.bfloat16),
            pltpu.VMEM((pieces, tms, blocks * per, rows), jnp.bfloat16),
            pltpu.VMEM((frames, inputs), jnp.float32),
            pltpu.VMEM((tms, frames, inputs), jnp.float32),
            pltpu.VMEM((2, tms * 2 * CH_DEV, STRIP), jnp.float32),
            pltpu.SemaphoreType.DMA,
            pltpu.SemaphoreType.DMA((pieces, strips)),
            pltpu.SemaphoreType.DMA((2, tms - 1)),
            pltpu.SemaphoreType.DMA((2, pieces, tms)),
            pltpu.SemaphoreType.DMA((2, pieces, inps - 1)),
        ],
        compiler_params=pltpu.CompilerParams(collective_id=0, has_side_effects=True, vmem_limit_bytes=60 << 20),
        name="channelize",
    )(fir, flags, samples)
    return pl.pallas_call(
        functools.partial(correlate, inps, (1.0 / (frames * tms), 2 * CH_DEV * tms)),
        out_shape=jax.ShapeDtypeStruct((CH_DEV, 2, inputs, inps * inputs), jnp.float32),
        in_specs=[vmem],
        out_specs=anywhere,
        scratch_shapes=[
            pltpu.VMEM((2, inputs, tms * per), jnp.float32),
            pltpu.VMEM((CH_DEV, 2, inputs, inps * inputs), jnp.float32),
            pltpu.SemaphoreType.DMA((CH_DEV, 2)),
        ],
        name="correlate",
    )(every)


def solution(mesh):
    in_specs = (P(("grp", "tm"), "inp", None), P(), P(("grp", "tm"), "inp"))
    out_specs = P(("grp", "tm"), None, "inp", None)
    return jax.shard_map(shards, mesh=mesh, in_specs=in_specs, out_specs=out_specs, check_vma=False)
```

time: 34.1 us -> 30.6 us (0.90)
  Pallas kernels: 33.9 us -> 30.4 us
    pallas_call x1, Pallas kernels: 29.9 us -> 27 us  [shards(): pl.pallas_call(functools.partial(channelize, tms, inps), out_shape=jax.Sh...]
    pallas_call x1, Pallas kernels: 4.04 us -> 3.34 us  [shards(): pl.pallas_call(functools.partial(correlate, inps, (1.0 / (frames * tms),...]
where the time goes in v1:
time: 30.6 us; the launch traced here: 30.4 us
  Pallas kernels  30.4 us (99%)
    pallas_call x1, Pallas kernels, shards(): pl.pallas_call(functools.partial(channelize, tms, inps), out_shape=jax.Sh...  27 us
    pallas_call x1, Pallas kernels, shards(): pl.pallas_call(functools.partial(correlate, inps, (1.0 / (frames * tms),...  3.34 us

profile of v1, /device:TPU:0, one launch (start us, length us, event | category | flops | bytes accessed | tf_op | source)
XLA Modules:
  0.0 30.4 jit_solution(13979576541537713511)
XLA Ops:
  0.0 27.0 %channelize.1.all_ref = bf16[4,128,256]{2,1,0:T(8,128)(2,1)} custom-call(f32[16,8192]{1,0:T(8,128)} %fir_hbm.1, s32[8,256]{1,0:T(8,128)} %flags_ref.1, bf16[8,256,8192]{2,1,0:T(8,128)(2,1)} %x_hbm.1), custom_call_target="tpu_custom_call" | custom-call | tf_op jit(solution)/shard_map/channelize/pallas_call | solution.py:210
  27.0 3.3 %correlate.1 = f32[2,2,256,1024]{3,2,1,0:T(8,128)} custom-call(bf16[4,128,256]{2,1,0:T(8,128)(2,1)} %channelize.1.all_ref), custom_call_target="tpu_custom_call" | custom-call | tf_op jit(solution)/shard_map/correlate/pallas_call | solution.py:234

commit v2 on v1

--- a/solution.py
+++ b/solution.py
@@ -10,7 +10,7 @@
 
 NCH = 4096
 CH_DEV = 2
-STRIP = 1024
+STRIP = 2048
 ROWS = 128
 
 

time: 30.6 us -> 29.5 us (0.964)
  Pallas kernels: 30.4 us -> 29.2 us
    pallas_call x1, Pallas kernels: 27 us -> 25.9 us  [shards(): pl.pallas_call(functools.partial(channelize, tms, inps), out_shape=jax.Sh...]
where the time goes in v2:
time: 29.5 us; the launch traced here: 29.2 us
  Pallas kernels  29.2 us (99%)
    pallas_call x1, Pallas kernels, shards(): pl.pallas_call(functools.partial(channelize, tms, inps), out_shape=jax.Sh...  25.9 us
    pallas_call x1, Pallas kernels, shards(): pl.pallas_call(functools.partial(correlate, inps, (1.0 / (frames * tms),...  3.34 us

profile of v2, /device:TPU:0, one launch (start us, length us, event | category | flops | bytes accessed | tf_op | source)
XLA Modules:
  0.0 29.2 jit_solution(11614900800880604188)
XLA Ops:
  0.0 25.9 %channelize.1.all_ref = bf16[4,128,256]{2,1,0:T(8,128)(2,1)} custom-call(f32[16,8192]{1,0:T(8,128)} %fir_hbm.1, s32[8,256]{1,0:T(8,128)} %flags_ref.1, bf16[8,256,8192]{2,1,0:T(8,128)(2,1)} %x_hbm.1), custom_call_target="tpu_custom_call" | custom-call | tf_op jit(solution)/shard_map/channelize/pallas_call | solution.py:210
  25.9 3.3 %correlate.1 = f32[2,2,256,1024]{3,2,1,0:T(8,128)} custom-call(bf16[4,128,256]{2,1,0:T(8,128)(2,1)} %channelize.1.all_ref), custom_call_target="tpu_custom_call" | custom-call | tf_op jit(solution)/shard_map/correlate/pallas_call | solution.py:234
